TPU v7x, 256 devices: a whole 4x4x8 slice. The times are simulated.
256 devices in a mesh: dp: 2 (over z_lo), seq: 16 (over y, x), tensor: 8 (over z_hi, core).
Axes of the slice: x: 4, y: 4, z: 8 (z_hi: 4, z_lo: 2; z = z_hi * 2 + z_lo), core: 2. Of those that a mesh axis runs over, the one named last changes fastest.
Arguments:
- query_rows: bfloat16 [2, 3072, 3072], P('dp', 'seq', 'tensor'), may hold values from -12 to 12
- key_rows: bfloat16 [2, 3072, 3072], P('dp', 'seq', 'tensor'), may hold values from -12 to 12
- value_rows: bfloat16 [2, 3072, 3072], P('dp', 'seq', 'tensor'), may hold values from -6 to 6
- lengths: int32 [2], P('dp'), may hold values from 1536 to 3072, as said below
- out_weight: bfloat16 [3072, 3072], P('seq', 'tensor'), may hold values from -4.1875 to 4.1875
- gate_vector: float32 [2, 3072], P('dp'), may hold values from 0.5 to 1.5
- cotangent: bfloat16 [2, 3072, 3072], P('dp', 'seq', 'tensor'), may hold values from -12 to 12
Outputs:
- branch_out: bfloat16 [2, 3072, 3072], P('dp', 'seq', 'tensor')
- grad_query: bfloat16 [2, 3072, 3072], P('dp', 'seq', 'tensor')
- grad_key: bfloat16 [2, 3072, 3072], P('dp', 'seq', 'tensor')
- grad_value: bfloat16 [2, 3072, 3072], P('dp', 'seq', 'tensor')
- grad_weight: float32 [3072, 3072], P('seq', 'tensor')
- grad_gate: float32 [2, 3072], P('dp', 'tensor')
Inputs may be any that keep to these rules, and one draw needn't show every extreme that they name: `lengths`: some clip has all 3072 positions live.
All inputs are finite; a program needn't handle non-finite values.
Results may differ from a plain program's by a relative error of at most 0.035.
Values may be sent and summed in bfloat16 or wider, within the bound.
A program may use at most 64 MiB of HBM per device.

v0:
```python
import math

import jax
import jax.numpy as jnp
from jax import lax
from jax.sharding import PartitionSpec as P

HD = 128


MASKED_SCORE = -1e30


def block_rows(piece_rows):
    return math.gcd(piece_rows, 512)


def query_terms(
    query_heads, grad_heads, row_lse, row_delta, key_block, value_block, key_live, score_scale
):
    scores = (
        jnp.einsum("thd,shd->ths", query_heads, key_block, preferred_element_type=jnp.float32)
        * score_scale
    )
    probs = jnp.where(key_live[None, None, :], jnp.exp(scores - row_lse[:, :, None]), 0.0)
    grad_probs = jnp.einsum(
        "thd,shd->ths", grad_heads, value_block, preferred_element_type=jnp.float32
    )
    dscores = (probs * (grad_probs - row_delta[:, :, None]) * score_scale).astype(jnp.bfloat16)
    return jnp.einsum("ths,shd->thd", dscores, key_block, preferred_element_type=jnp.float32)


def key_terms(
    query_block, grad_block, lse_block, delta_block, key_heads, value_heads, key_live, score_scale
):
    scores = (
        jnp.einsum("shd,thd->sht", query_block, key_heads, preferred_element_type=jnp.float32)
        * score_scale
    )
    probs = jnp.where(key_live[None, None, :], jnp.exp(scores - lse_block[:, :, None]), 0.0)
    value_part = jnp.einsum(
        "sht,shd->thd", probs.astype(jnp.bfloat16), grad_block, preferred_element_type=jnp.float32
    )
    grad_probs = jnp.einsum(
        "shd,thd->sht", grad_block, value_heads, preferred_element_type=jnp.float32
    )
    dscores = (probs * (grad_probs - delta_block[:, :, None]) * score_scale).astype(jnp.bfloat16)
    key_part = jnp.einsum("sht,shd->thd", dscores, query_block, preferred_element_type=jnp.float32)
    return (key_part, value_part)


def shards(query_rows, key_rows, value_rows, lengths, out_weight, gate_vector, cotangent):
    tokens = query_rows.shape[1]
    local_width = query_rows.shape[2]
    head_count = local_width // HD
    score_scale = 1.0 / math.sqrt(HD)
    length = lengths[0]
    query_local = query_rows[0]
    key_local = key_rows[0]
    value_local = value_rows[0]
    query_heads = query_local.reshape(tokens, head_count, HD)
    key_heads = key_local.reshape(tokens, head_count, HD)
    value_heads = value_local.reshape(tokens, head_count, HD)
    head_zeros = jnp.zeros((tokens, head_count, HD), jnp.float32)
    start_top = jnp.full((tokens, head_count), MASKED_SCORE, jnp.float32)
    start_total = jnp.zeros((tokens, head_count), jnp.float32)
    key_piece = lax.all_gather(key_local, "seq", axis=0, tiled=True)
    value_piece = lax.all_gather(value_local, "seq", axis=0, tiled=True)
    piece_rows = key_piece.shape[0]
    step_rows = block_rows(piece_rows)

    def forward_block_step(block_index, state):
        row_top, row_total, summed = state
        offset = block_index * step_rows
        key_block = lax.dynamic_slice_in_dim(key_piece, offset, step_rows, 0).reshape(
            step_rows, head_count, HD
        )
        value_block = lax.dynamic_slice_in_dim(value_piece, offset, step_rows, 0).reshape(
            step_rows, head_count, HD
        )
        key_live = offset + jnp.arange(step_rows) < length
        scores = (
            jnp.einsum("thd,shd->ths", query_heads, key_block, preferred_element_type=jnp.float32)
            * score_scale
        )
        masked = jnp.where(key_live[None, None, :], scores, MASKED_SCORE)
        new_top = jnp.maximum(row_top, jnp.max(masked, axis=2))
        weights = jnp.where(key_live[None, None, :], jnp.exp(masked - new_top[:, :, None]), 0.0)
        shrink = jnp.exp(row_top - new_top)
        row_total = row_total * shrink + jnp.sum(weights, axis=2)
        summed = summed * shrink[:, :, None] + jnp.einsum(
            "ths,shd->thd",
            weights.astype(jnp.bfloat16),
            value_block,
            preferred_element_type=jnp.float32,
        )
        return (new_top, row_total, summed)

    row_top, row_total, summed = lax.fori_loop(
        0, piece_rows // step_rows, forward_block_step, (start_top, start_total, head_zeros)
    )
    attended_heads = (summed / row_total[:, :, None]).astype(jnp.bfloat16)
    attended = attended_heads.reshape(tokens, local_width)
    row_lse = row_top + jnp.log(row_total)
    weight_whole = lax.all_gather(out_weight, "seq", axis=0, tiled=True)
    partial_value = jnp.einsum(
        "tk,rk->tr", attended, weight_whole, preferred_element_type=jnp.float32
    )
    projected = lax.psum_scatter(
        partial_value.astype(jnp.bfloat16), "tensor", scatter_dimension=1, tiled=True
    ).astype(jnp.float32)
    out_width = projected.shape[1]
    gate_local = lax.dynamic_slice_in_dim(
        gate_vector[0], lax.axis_index("tensor") * out_width, out_width
    )
    cot_rows = cotangent[0].astype(jnp.float32)
    branch = (gate_local[None, :] * projected).astype(jnp.bfloat16)
    gate_grad = lax.psum(jnp.sum(cot_rows * projected, axis=0), "seq")
    grad_proj = (gate_local[None, :] * cot_rows).astype(jnp.bfloat16)
    grad_full = lax.all_gather(grad_proj, "tensor", axis=1, tiled=True)
    grad_att = jnp.dot(grad_full, weight_whole, preferred_element_type=jnp.float32).astype(
        jnp.bfloat16
    )
    row_share = lax.psum_scatter(
        jnp.einsum("tr,tk->rk", grad_full, attended, preferred_element_type=jnp.float32).astype(
            jnp.bfloat16
        ),
        "seq",
        scatter_dimension=0,
        tiled=True,
    )
    grad_weight = lax.psum(row_share, "dp").astype(jnp.float32)
    grad_heads = grad_att.reshape(tokens, head_count, HD)
    row_delta = jnp.sum(grad_heads.astype(jnp.float32) * attended_heads.astype(jnp.float32), axis=2)
    all_lse, all_delta = (
        lax.all_gather(row_lse, "seq", axis=0, tiled=True),
        lax.all_gather(row_delta, "seq", axis=0, tiled=True),
    )
    key_offset = lax.axis_index("seq") * tokens
    local_live = key_offset + jnp.arange(tokens) < length
    query_key_piece = lax.all_gather(key_local, "seq", axis=0, tiled=True)
    query_value_piece = lax.all_gather(value_local, "seq", axis=0, tiled=True)
    piece_rows = query_key_piece.shape[0]
    query_step_rows = block_rows(piece_rows)

    def query_block_step(block_index, state):
        offset = block_index * query_step_rows
        key_block = lax.dynamic_slice_in_dim(query_key_piece, offset, query_step_rows, 0).reshape(
            query_step_rows, head_count, HD
        )
        value_block = lax.dynamic_slice_in_dim(
            query_value_piece, offset, query_step_rows, 0
        ).reshape(query_step_rows, head_count, HD)
        key_live = offset + jnp.arange(query_step_rows) < length
        return state + query_terms(
            query_heads,
            grad_heads,
            row_lse,
            row_delta,
            key_block,
            value_block,
            key_live,
            score_scale,
        )

    grad_q = lax.fori_loop(0, piece_rows // query_step_rows, query_block_step, head_zeros)
    query_piece = lax.all_gather(query_local, "seq", axis=0, tiled=True)
    grad_piece = lax.all_gather(grad_att, "seq", axis=0, tiled=True)
    piece_rows = query_piece.shape[0]
    key_step_rows = block_rows(piece_rows)

    def key_block_step(block_index, state):
        offset = block_index * key_step_rows
        query_block = lax.dynamic_slice_in_dim(query_piece, offset, key_step_rows, 0).reshape(
            key_step_rows, head_count, HD
        )
        grad_block = lax.dynamic_slice_in_dim(grad_piece, offset, key_step_rows, 0).reshape(
            key_step_rows, head_count, HD
        )
        lse_block = lax.dynamic_slice_in_dim(all_lse, offset, key_step_rows, 0)
        delta_block = lax.dynamic_slice_in_dim(all_delta, offset, key_step_rows, 0)
        key_part, value_part = key_terms(
            query_block,
            grad_block,
            lse_block,
            delta_block,
            key_heads,
            value_heads,
            local_live,
            score_scale,
        )
        return (state[0] + key_part, state[1] + value_part)

    grad_k, grad_v = lax.fori_loop(
        0, piece_rows // key_step_rows, key_block_step, (head_zeros, head_zeros)
    )
    grad_query = grad_q.reshape(tokens, local_width).astype(jnp.bfloat16)
    grad_key = grad_k.reshape(tokens, local_width).astype(jnp.bfloat16)
    grad_value = grad_v.reshape(tokens, local_width).astype(jnp.bfloat16)
    return (
        branch[None],
        grad_query[None],
        grad_key[None],
        grad_value[None],
        grad_weight,
        gate_grad[None],
    )


def solution(mesh):
    placed = (
        P("dp", "seq", "tensor"),
        P("dp", "seq", "tensor"),
        P("dp", "seq", "tensor"),
        P("dp"),
        P("seq", "tensor"),
        P("dp", None),
        P("dp", "seq", "tensor"),
    )
    return jax.shard_map(
        shards,
        mesh=mesh,
        in_specs=placed,
        out_specs=(
            P("dp", "seq", "tensor"),
            P("dp", "seq", "tensor"),
            P("dp", "seq", "tensor"),
            P("dp", "seq", "tensor"),
            P("seq", "tensor"),
            P("dp", "tensor"),
        ),
        check_vma=False,
    )
```

profile of v0, /device:TPU:1, one launch (start us, length us, event | category | flops | bytes accessed | tf_op | source)
XLA Modules:
  0.0 500.3 jit_solution(13584683113737516076)
XLA Ops:
  7.9 1.6 fusion.49
  12.7 32.8 %all-gather.14.cloned.1.call-done = bf16[192,3072]{1,0:T(8,128)(2,1)} async-done(((bf16[192,384]{1,0:T(8,128)(2,1)}), bf16[192,3072]{1,0:T(8,128)(2,1)}) %all-gather.14.cloned.1.call-update) | async-done | bytes 1179664 | tf_op jit(solution)/shard_map/all_gather | solution.py:120
  45.5 49.8 %all-gather.12.cloned.1.call-done = bf16[3072,384]{1,0:T(8,128)(2,1)} async-done(((bf16[192,384]{1,0:T(8,128)(2,1)}), bf16[3072,384]{1,0:T(8,128)(2,1)}) %all-gather.12.cloned.1.call-update) | async-done | bytes 2359312 | tf_op jit(solution)/shard_map/all_gather | solution.py:105
  95.2 2.8 convolution_convert_fusion.2
  98.1 49.7 %all-gather.18.cloned.1.call-done = bf16[1,3072,384]{2,1,0:T(8,128)(2,1)} async-done(((bf16[1,192,384]{2,1,0:T(8,128)(2,1)}), bf16[1,3072,384]{2,1,0:T(8,128)(2,1)}) %all-gather.18.cloned.1.call-update) | async-done | bytes 2359312 | tf_op jit(solution)/shard_map/all_gather | solution.py:67
  147.8 4.3 copy.76
  152.1 48.1 %all-gather.20.cloned.1.call-done = bf16[1,3072,384]{2,1,0:T(8,128)(2,1)} async-done(((bf16[1,192,384]{2,1,0:T(8,128)(2,1)}), bf16[1,3072,384]{2,1,0:T(8,128)(2,1)}) %all-gather.20.cloned.1.call-update) | async-done | bytes 2359312 | tf_op jit(solution)/shard_map/all_gather | solution.py:68
  200.2 4.3 copy.78
  204.5 18.5 %while.48 = (s32[]{:T(128)}, f32[192,3]{0,1:T(4,128)S(1)}, f32[192,3]{0,1:T(4,128)S(1)}, f32[192,3,128]{2,0,1:T(8,128)S(1)}, s32[]{:T(128)}, /*index=5*/bf16[307...) while((s32[]{:T(128)}, f32[192,3]{0,1:T(4,128)S(1)}, ...), condition=%wide.region_3.4_spmd.clone, body=%wide.region_0.3_spmd.clone.sunk | while | flops 153874240 | bytes 6674627 | solution.py:99
  223.7 2.6 convolution_convert_fusion.1
  226.3 1.6 copy.105
  228.0 1.2 copy-done.2
  229.2 2.4 convolution_convert_fusion
  233.2 17.2 %while.49 = (s32[]{:T(128)}, f32[192,3,128]{2,0,1:T(8,128)S(1)}, bf16[3072,384]{0,1:T(8,128)(2,1)}, s32[]{:T(128)}, bf16[192,3,128]{2,0,1:T(8,128)(2,1)S(1)}, /*...) while((s32[]{:T(128)}, f32[192,3,128]{2,0,1:T(8,128)S(1)}, ...), condition=%wide.region_7.8_spmd.clone, body=%wide.region_6.7_spmd.clone.sunk | while | flops 228705280 | bytes 5609161 | solution.py:166
  238.9 1.2 constant_dynamic-slice_fusion.13
  244.7 1.2 constant_dynamic-slice_fusion.13
  247.5 1.2 constant_dynamic-slice_fusion.13
  251.4 17.8 %all-gather.3 = f32[16,192,3]{1,2,0:T(4,128)S(1)} all-gather(f32[1,192,3]{1,2,0:T(4,128)S(1)} %bitcast.191), channel_id=1, replica_groups=mesh['dp'=2,'seq'=16,'tensor'=8] {'seq'}, dimensions={0}, use_global_device_ids=true | all-gather | bytes 39168 | tf_op jit(solution)/shard_map/all_gather | solution.py:136
  269.4 17.2 %all-gather.4 = f32[16,192,3]{1,2,0:T(4,128)S(1)} all-gather(f32[1,192,3]{1,2,0:T(4,128)S(1)} %copy.88), channel_id=1, replica_groups=mesh['dp'=2,'seq'=16,'tensor'=8] {'seq'}, dimensions={0}, use_global_device_ids=true | all-gather | bytes 39168 | tf_op jit(solution)/shard_map/all_gather | solution.py:137
  288.5 31.6 %psum.15 = f32[1,384]{1,0:T(1,128)} all-reduce(f32[1,384]{1,0:T(1,128)S(1)} %broadcast_in_dim.137), channel_id=1, replica_groups=mesh['dp'=2,'seq'=16,'tensor'=8] {'seq'}, use_global_device_ids=true, to_apply=%region_13.14 | all-reduce | flops 384 | bytes 3072 | tf_op jit(solution)/shard_map/psum | solution.py:118
  320.1 30.2 %reduce-scatter.5.cloned.1.call-done = bf16[192,384]{1,0:T(8,128)(2,1)} async-done(((bf16[3072,384]{1,0:T(8,128)(2,1)}), bf16[192,384]{1,0:T(8,128)(2,1)}) %reduce-scatter.5.cloned.1.call-update) | async-done | bytes 147472 | tf_op jit(solution)/shard_map/reduce_scatter | solution.py:124
  350.3 53.2 %all-gather.22.cloned.1.call-done = bf16[1,3072,384]{2,1,0:T(8,128)(2,1)} async-done(((bf16[1,192,384]{2,1,0:T(8,128)(2,1)}), bf16[1,3072,384]{2,1,0:T(8,128)(2,1)}) %all-gather.22.cloned.1.call-update) | async-done | bytes 2359312 | tf_op jit(solution)/shard_map/all_gather | solution.py:167
  403.5 53.1 %all-gather.16.cloned.1.call-done = bf16[3072,384]{1,0:T(8,128)(2,1)} async-done(((bf16[192,384]{1,0:T(8,128)(2,1)}), bf16[3072,384]{1,0:T(8,128)(2,1)}) %all-gather.16.cloned.1.call-update) | async-done | bytes 2359312 | tf_op jit(solution)/shard_map/all_gather | solution.py:168
  456.7 21.0 %while.50 = (s32[]{:T(128)}, f32[192,3,128]{2,0,1:T(8,128)S(1)}, f32[192,3,128]{2,0,1:T(8,128)S(1)}, bf16[3072,384]{1,0:T(8,128)(2,1)}, bf16[192,3,128]{2,0,1:T(...) while((s32[]{:T(128)}, f32[192,3,128]{2,0,1:T(8,128)S(1)}, ...), condition=%wide.region_9.10_spmd.clone, body=%wide.region_8.9_spmd.clone.sunk | while | flops 304644480 | bytes 9769566 | solution.py:194
  456.7 1.2 constant_dynamic-slice_fusion.14
  460.2 1.2 constant_dynamic-slice_fusion.14
  463.7 1.2 constant_dynamic-slice_fusion.14
  467.2 1.2 constant_dynamic-slice_fusion.14
  470.7 1.2 constant_dynamic-slice_fusion.14
  474.2 1.2 constant_dynamic-slice_fusion.14
  479.6 12.5 %all-reduce.2.cloned.1.call-done = bf16[192,384]{1,0:T(8,128)(2,1)} async-done(((bf16[192,384]{1,0:T(8,128)(2,1)}), bf16[192,384]{1,0:T(8,128)(2,1)}) %all-reduce.2.cloned.1.call-update) | async-done | bytes 147472 | tf_op jit(solution)/shard_map/psum | solution.py:132
  492.1 1.6 convert_element_type.120
  (177 shorter events, 55.8 us)
Async XLA Ops:
  7.2 0.7 copy-start
  7.2 38.3 %all-gather.14.cloned.1.call-start = ((), (), s32[]{:S(2)}) async-start(), calls=%async_computation.3 | async-start | bytes 1327104 | tf_op jit(solution)/shard_map/all_gather | solution.py:120
  9.5 85.7 %all-gather.12.cloned.1.call-start = ((), (), s32[]{:S(2)}) async-start(), calls=%async_computation.2 | async-start | bytes 2506752 | tf_op jit(solution)/shard_map/all_gather | solution.py:105
  10.3 137.5 %all-gather.18.cloned.1.call-start = ((), (), s32[]{:S(2)}) async-start(), calls=%async_computation.7 | async-start | bytes 2506752 | tf_op jit(solution)/shard_map/all_gather | solution.py:67
  11.0 189.2 %all-gather.20.cloned.1.call-start = ((), (), s32[]{:S(2)}) async-start(), calls=%async_computation.8 | async-start | bytes 2506752 | tf_op jit(solution)/shard_map/all_gather | solution.py:68
  11.6 275.1 %reduce-scatter.7.cloned.1.call-start = ((), (), s32[]{:S(2)}) async-start(), calls=%async_computation.10 | async-start | bytes 1769472
  98.0 134.8 %copy-start.1 = (bf16[192,384]{1,0:T(8,128)(2,1)}, bf16[192,384]{1,0:T(8,128)(2,1)S(1)}, u32[]{:S(2)}) copy-start(bf16[192,384]{1,0:T(8,128)(2,1)S(1)} %convolution_convert_fusion.2) | copy-start | bytes 442372
  227.9 1.3 copy-start.2
  228.0 122.3 %reduce-scatter.5.cloned.1.call-start = ((), (), s32[]{:S(2)}) async-start(), calls=%async_computation.5 | async-start | bytes 2506752 | tf_op jit(solution)/shard_map/reduce_scatter | solution.py:124
  231.6 0.9 copy-start.4
  231.6 1.0 copy-start.5
  231.6 171.9 %all-gather.22.cloned.1.call-start = ((), (), s32[]{:S(2)}) async-start(), calls=%async_computation.9 | async-start | bytes 2506752 | tf_op jit(solution)/shard_map/all_gather | solution.py:167
  232.4 224.3 %all-gather.16.cloned.1.call-start = ((), (), s32[]{:S(2)}) async-start(), calls=%async_computation.4 | async-start | bytes 2506752 | tf_op jit(solution)/shard_map/all_gather | solution.py:168
  233.1 259.0 %all-reduce.2.cloned.1.call-start = ((), (), s32[]{:S(2)}) async-start(), calls=%async_computation.6 | async-start | bytes 294912 | tf_op jit(solution)/shard_map/psum | solution.py:132
  250.4 37.4 %copy-start.3 = (bf16[1,192,384]{2,1,0:T(8,128)(2,1)S(1)}, bf16[1,192,384]{2,1,0:T(8,128)(2,1)}, u32[]{:S(2)}) copy-start(bf16[1,192,384]{2,1,0:T(8,128)(2,1)} %param.19) | copy-start | bytes 442372
Sparse Core Ops, SparseCore 0:
  10.4 34.9 all-gather.13
  47.9 47.2 all-gather.11
  97.6 50.0 all-gather.17
  150.1 50.0 all-gather.19
  228.1 40.1 reduce-scatter.6
  271.7 78.5 reduce-scatter.4
  352.7 50.7 all-gather.21
  406.5 50.0 all-gather.15
  459.2 32.8 all-reduce.1
where the time goes:
time: 501 us; the launch traced here: 500 us
  waiting for transfers between devices  332 us (66%)
  blocking collectives  66.6 us (13%)
  local copies, waits for them, and re-layouts  41.4 us (8%)
  matrix products  25.5 us (5%)
  other arithmetic  18.9 us (4%)
  between operations  14.1 us (3%)
    all_gather x1, waiting for transfers between devices, shards(): query_piece = lax.all_gather(query_local, 'seq', axis=0, tiled=True)  53.2 us
    all_gather x1, waiting for transfers between devices, shards(): grad_piece = lax.all_gather(grad_att, 'seq', axis=0, tiled=True)  53.1 us
    all_gather x1, waiting for transfers between devices, shards(): weight_whole = lax.all_gather(out_weight, 'seq', axis=0, tiled=True)  49.8 us
    all_gather x1, waiting for transfers between devices, shards(): key_piece = lax.all_gather(key_local, 'seq', axis=0, tiled=True)  49.7 us
    all_gather x1, waiting for transfers between devices, shards(): value_piece = lax.all_gather(value_local, 'seq', axis=0, tiled=True)  48.1 us
    all_gather x1, waiting for transfers between devices, shards(): grad_full = lax.all_gather(grad_proj, 'tensor', axis=1, tiled=True)  32.8 us
    psum x1, blocking collectives, shards(): gate_grad = lax.psum(jnp.sum(cot_rows * projected, axis=0), 'seq')  31.6 us
    reduce_scatter x1, waiting for transfers between devices, shards(): lax.psum_scatter(jnp.einsum('tr,tk->rk', grad_full, attended, preferred_e...  30.2 us
  transfers between devices with their start and end apart: 9, of which 8 were waited for; matrix products, arithmetic and copies ran while one was open for 11% of the time, Pallas kernels for 0%

commit v1 on v0

v1 whole, which is shorter than its diff:
```python
import functools
import math

import jax
import jax.numpy as jnp
from jax import lax
from jax.experimental import pallas as pl
from jax.experimental.pallas import tpu as pltpu
from jax.sharding import PartitionSpec as P

HD = 128
NX = 4
NY = 4
NZ = 4
MASKED = -1e30
MESH = pl.DeviceIdType.MESH
BF = jnp.bfloat16
F32 = jnp.float32


def dot_nn(a, b):
    return lax.dot_general(a, b, (((1,), (0,)), ((), ())), preferred_element_type=F32)


def dot_nt(a, b):
    return lax.dot_general(a, b, (((1,), (1,)), ((), ())), preferred_element_type=F32)


def dot_tn(a, b):
    return lax.dot_general(a, b, (((0,), (0,)), ((), ())), preferred_element_type=F32)


SEMS = {}
SEM_COUNT = 0
for sem_name, sem_size in (
    ("wa1", 3), ("wb1", 3), ("wa2", 3), ("wb2", 3), ("q", 3), ("k", 3), ("v", 3),
    ("gz", 3), ("gc", 1), ("gf", 3), ("o", 9), ("st", 3), ("do", 3), ("pc", 1), ("pz", 3),
    ("wx1", 3), ("wy1", 3), ("wx2", 3), ("wy2", 3), ("wd", 1), ("dl", 3),
    ("dk", 9), ("dv", 9), ("dq", 9), ("gx", 3), ("gy", 3),
):
    SEMS[sem_name] = SEM_COUNT
    SEM_COUNT += sem_size


def kernel(
    len_ref, q_ref, k_ref, v_ref, w_ref, gate_ref, cot_ref,
    br_ref, gq_ref, gk_ref, gv_ref, gw_ref, gg_ref,
    qbuf, kbuf, vbuf, gfull, wfull, scores, pbuf, top, stat, lse, wrow, wcol,
    osend, orecv, att, dobuf, dacc, psib, psrecv, pown, pzsend, pzrecv,
    dw, wxr, wyr, wxs, wys, wx2r, wy2r, wdsend, wdrecv, dls, delta,
    dks, dkr, dvs, dvr, dqs, dqr, dqacc, gxb, gyb,
    ss, rs,
):
    T = q_ref.shape[0]
    DL = q_ref.shape[1]
    NH = DL // HD
    Q = NX * T
    RA = T // 3
    scale = 1.0 / math.sqrt(HD)
    seq = lax.axis_index("seq")
    ten = lax.axis_index("tensor")
    dp = lax.axis_index("dp")
    x = lax.rem(seq, NX)
    y = lax.div(seq, NX)
    zh = lax.div(ten, 2)
    c = lax.rem(ten, 2)

    def xi(d):
        return lax.rem(x + d, NX)

    def yi(d):
        return lax.rem(y + d, NY)

    def zi(d):
        return lax.rem(zh + d, NZ)

    def X(d):
        return {"seq": y * NX + xi(d)}

    def Y(d):
        return {"seq": yi(d) * NX + x}

    def Z(d):
        return {"tensor": zi(d) * 2 + c}

    sibling = {"tensor": zh * 2 + 1 - c}
    twin = {"dp": 1 - dp}

    def rc(name, i, src, dst, peer):
        j = SEMS[name] + i
        return pltpu.make_async_remote_copy(
            src_ref=src, dst_ref=dst, send_sem=ss.at[j], recv_sem=rs.at[j],
            device_id=peer, device_id_type=MESH,
        )

    sent = []

    def go(*args):
        copy = rc(*args)
        copy.start()
        sent.append(copy)
        return copy

    def lanes(h):
        return pl.ds(pl.multiple_of(h * HD, HD), HD)

    barrier = pltpu.get_barrier_semaphore()
    peers = [X(d) for d in (1, 2, 3)] + [Y(d) for d in (1, 2, 3)] + [Z(d) for d in (1, 2, 3)]
    peers += [sibling, twin]
    for peer in peers:
        pl.semaphore_signal(barrier, inc=1, device_id=peer, device_id_type=MESH)
    gate_local = gate_ref[:, pl.ds(pl.multiple_of(ten * DL, HD), DL)]
    gfull[ten] = (gate_local * cot_ref[...].astype(F32)).astype(BF)
    qbuf[x] = q_ref[...]
    kbuf[y] = k_ref[...]
    vbuf[y] = v_ref[...]
    wfull[y, x] = w_ref[...]
    wrow[...] = jnp.zeros_like(wrow)
    pl.semaphore_wait(barrier, len(peers))

    wa1 = [go("wa1", d - 1, w_ref.at[0:RA], wfull.at[y, x, 0:RA], X(d)) for d in (1, 2, 3)]
    wb1 = [go("wb1", d - 1, w_ref.at[RA:T], wfull.at[y, x, RA:T], Y(d)) for d in (1, 2, 3)]
    q_in = [go("q", d - 1, q_ref, qbuf.at[x], X(d)) for d in (1, 2, 3)]
    k_in = [go("k", d - 1, k_ref, kbuf.at[y], Y(d)) for d in (1, 2, 3)]
    v_in = [go("v", d - 1, v_ref, vbuf.at[y], Y(d)) for d in (1, 2, 3)]
    g_in = [go("gz", d - 1, gfull.at[ten], gfull.at[ten], Z(d)) for d in (1, 2, 3)]
    g_sib = go("gc", 0, gfull.at[ten], gfull.at[ten], sibling)

    for copy in wa1:
        copy.wait_recv()
    wa2 = [go("wa2", d - 1, wfull.at[y, :, 0:RA], wfull.at[y, :, 0:RA], Y(d)) for d in (1, 2, 3)]
    for copy in wb1:
        copy.wait_recv()
    wb2 = [go("wb2", d - 1, wfull.at[:, x, RA:T], wfull.at[:, x, RA:T], X(d)) for d in (1, 2, 3)]

    for copy in q_in:
        copy.wait_recv()
    length = len_ref[0]
    top[...] = jnp.full_like(top, MASKED)

    def score_block(j):
        rows = (j * NX + x) * T + lax.broadcasted_iota(jnp.int32, (T, 1), 0)
        live = rows < length

        def head(h, carry):
            s = dot_nt(kbuf[j, :, lanes(h)], qbuf[:, :, lanes(h)].reshape(Q, HD)) * scale
            s = jnp.where(live, s, MASKED)
            scores[h, j] = s
            top[pl.ds(h, 1), :] = jnp.maximum(
                top[pl.ds(h, 1), :], jnp.max(s, axis=0, keepdims=True)
            )
            return carry

        lax.fori_loop(0, NH, head, 0)

    score_block(y)
    for d in (3, 1, 2):
        k_in[d - 1].wait_recv()
        score_block(yi(NY - d))

    g_fwd = []
    for d in (1, 3, 2):
        g_in[d - 1].wait_recv()
        t = zi(NZ - d) * 2 + c
        g_fwd.append(go("gf", d - 1, gfull.at[t], gfull.at[t], sibling))

    for copy in v_in:
        copy.wait_recv()

    stat[x] = jnp.zeros((8, Q), F32)

    def forward_head(h, carry):
        row_top = top[pl.ds(h, 1), :]

        def block(j, total):
            p = jnp.exp(scores[h, j] - row_top)
            pbuf[j] = p.astype(BF)
            return total + jnp.sum(p, axis=0, keepdims=True)

        total = lax.fori_loop(0, NY, block, jnp.zeros((1, Q), F32))
        out_t = dot_tn(vbuf[:, :, lanes(h)].reshape(Q, HD), pbuf[...].reshape(Q, Q))
        out_t = out_t / total
        osend[:, :, lanes(h)] = out_t.T.astype(BF).reshape(NX, T, HD)
        stat[x, pl.ds(h, 1), :] = row_top + jnp.log(total)
        for d in (1, 2, 3):
            rc(
                "o", h * 3 + d - 1, osend.at[xi(d), :, lanes(h)],
                orecv.at[x, :, lanes(h)], X(d),
            ).start()
        return carry

    lax.fori_loop(0, NH, forward_head, 0)
    st_in = [go("st", d - 1, stat.at[x], stat.at[x], X(d)) for d in (1, 2, 3)]
    orecv[x] = osend[x]

    for copy in wa2 + wb2 + g_fwd + [g_sib]:
        copy.wait_recv()

    def weight_rows(t):
        return wfull[lax.div(t, 2), pl.ds(lax.rem(t, 2) * 2, 2)].reshape(2 * T, DL)

    dacc[...] = jnp.zeros_like(dacc)

    def grad_step(t, carry):
        dacc[...] += dot_nn(gfull[t], weight_rows(t))
        return carry

    lax.fori_loop(0, 2 * NZ, grad_step, 0)
    dobuf[x] = dacc[...].astype(BF)
    do_in = [go("do", d - 1, dobuf.at[x], dobuf.at[x], X(d)) for d in (1, 2, 3)]

    for copy in st_in:
        copy.wait_recv()
    for h in range(NH):
        parts = [stat[j, h : h + 1, :] for j in range(NX)]
        high = functools.reduce(jnp.maximum, parts)
        row_lse = high + jnp.log(sum(jnp.exp(part - high) for part in parts))
        lse[h : h + 1, :] = row_lse
        for j in range(NX):
            wrow[h * NX + j : h * NX + j + 1, :] = jnp.exp(parts[j] - row_lse)
    wcol[...] = wrow[...].T

    def o_copy(h, d):
        return rc(
            "o", h * 3 + d - 1, osend.at[xi(d), :, lanes(h)], orecv.at[x, :, lanes(h)], X(d)
        )

    def wait_o(h, carry):
        for d in (1, 2, 3):
            o_copy(h, d).wait_recv()
        return carry

    lax.fori_loop(0, NH, wait_o, 0)
    weights = wcol[pl.ds(pl.multiple_of(x * T, 64), T), :]
    for h in range(NH):
        total = jnp.zeros((T, HD), F32)
        for j in range(NX):
            col = h * NX + j
            total += weights[:, col : col + 1] * orecv[j, :, h * HD : (h + 1) * HD].astype(F32)
        att[:, h * HD : (h + 1) * HD] = total.astype(BF)

    def proj_sib(z, carry):
        rows = wfull[z, pl.ds((1 - c) * 2, 2)].reshape(2 * T, DL)
        psib[z] = dot_nt(att[...], rows).astype(BF)
        return carry

    lax.fori_loop(0, NZ, proj_sib, 0)
    p_sib = go("pc", 0, psib, psrecv, sibling)

    def weight_grad(t, carry):
        part = dot_tn(gfull[t], att[...]).astype(BF).reshape(2, T, DL)
        dw[lax.div(t, 2), pl.ds(lax.rem(t, 2) * 2, 2)] = part
        return carry

    lax.fori_loop(0, 2 * NZ, weight_grad, 0)
    wx1 = [go("wx1", d - 1, dw.at[:, xi(d), 0:RA], wxr.at[d - 1], X(d)) for d in (1, 2, 3)]
    wy1 = [go("wy1", d - 1, dw.at[yi(d), :, RA:T], wyr.at[d - 1], Y(d)) for d in (1, 2, 3)]

    def proj_own(z, carry):
        rows = wfull[z, pl.ds(c * 2, 2)].reshape(2 * T, DL)
        pown[z] = dot_nt(att[...], rows)
        return carry

    lax.fori_loop(0, NZ, proj_own, 0)
    p_sib.wait_recv()

    def proj_add(z, carry):
        value = pown[z] + psrecv[z].astype(F32)
        pown[z] = value
        pzsend[z] = value.astype(BF)
        return carry

    lax.fori_loop(0, NZ, proj_add, 0)
    pz = [go("pz", d - 1, pzsend.at[zi(d)], pzrecv.at[d - 1], Z(d)) for d in (1, 2, 3)]

    for copy in do_in:
        copy.wait_recv()
    ones = jnp.ones((8, HD), F32)
    dls[x] = jnp.zeros((8, Q), F32)
    for h in range(NH):
        sl = slice(h * HD, (h + 1) * HD)
        prod = dobuf[:, :, sl].astype(F32) * osend[:, :, sl].astype(F32)
        rows = lax.dot_general(
            ones, prod.reshape(Q, HD), (((1,), (1,)), ((), ())),
            preferred_element_type=F32, precision=lax.Precision.HIGHEST,
        )
        dls[x, h : h + 1, :] = rows[0:1, :]
    dl_in = [go("dl", d - 1, dls.at[x], dls.at[x], X(d)) for d in (1, 2, 3)]
    for copy in dl_in:
        copy.wait_recv()
    for h in range(NH):
        delta[h : h + 1, :] = sum(
            wrow[h * NX + j : h * NX + j + 1, :] * dls[j, h : h + 1, :] for j in range(NX)
        )

    def kv_copy(name, h, d, src, dst):
        return rc(
            name, h * 3 + d - 1, src.at[yi(d), :, lanes(h)], dst.at[d - 1, :, lanes(h)], Y(d)
        )

    def q_copy(h, d):
        return rc("dq", h * 3 + d - 1, dqs.at[xi(d), :, lanes(h)], dqr.at[d - 1, :, lanes(h)], X(d))

    def backward_head(h, carry):
        row_lse = lse[pl.ds(h, 1), :]
        row_delta = delta[pl.ds(h, 1), :]
        dqacc[...] = jnp.zeros_like(dqacc)
        for d in (1, 2, 3, 0):
            j = yi(d)
            grads = dobuf[:, :, lanes(h)].reshape(Q, HD)
            p = jnp.exp(scores[h, j] - row_lse)
            dp_t = dot_nt(vbuf[j, :, lanes(h)], grads)
            ds = (p * (dp_t - row_delta) * scale).astype(BF)
            dvs[j, :, lanes(h)] = dot_nn(p.astype(BF), grads).astype(BF)
            dks[j, :, lanes(h)] = dot_nn(ds, qbuf[:, :, lanes(h)].reshape(Q, HD)).astype(BF)
            if d:
                kv_copy("dv", h, d, dvs, dvr).start()
                kv_copy("dk", h, d, dks, dkr).start()
            dqacc[...] += dot_tn(kbuf[j, :, lanes(h)], ds)
        dqs[:, :, lanes(h)] = dqacc[...].T.astype(BF).reshape(NX, T, HD)
        for d in (1, 2, 3):
            q_copy(h, d).start()
        return carry

    lax.fori_loop(0, NH, backward_head, 0)

    for copy in wx1:
        copy.wait_recv()

    def sum_x(j, carry):
        total = dw[j, x, 0:RA].astype(F32)
        for d in (1, 2, 3):
            total += wxr[d - 1, j].astype(F32)
        wxs[j] = total.astype(BF)
        return carry

    lax.fori_loop(0, NY, sum_x, 0)
    wx2 = [go("wx2", d - 1, wxs.at[yi(d)], wx2r.at[d - 1], Y(d)) for d in (1, 2, 3)]
    for copy in wy1:
        copy.wait_recv()

    def sum_y(j, carry):
        total = dw[y, j, RA:T].astype(F32)
        for d in (1, 2, 3):
            total += wyr[d - 1, j].astype(F32)
        wys[j] = total.astype(BF)
        return carry

    lax.fori_loop(0, NX, sum_y, 0)
    wy2 = [go("wy2", d - 1, wys.at[xi(d)], wy2r.at[d - 1], X(d)) for d in (1, 2, 3)]

    for copy in pz:
        copy.wait_recv()
    projected = pown[zh]
    for d in (1, 2, 3):
        projected += pzrecv[d - 1].astype(F32)
    br_ref[...] = (gate_local * projected).astype(BF)
    gxb[x] = jnp.broadcast_to(
        jnp.sum(cot_ref[...].astype(F32) * projected, axis=0, keepdims=True), (8, DL)
    )
    gx = [go("gx", d - 1, gxb.at[x], gxb.at[x], X(d)) for d in (1, 2, 3)]

    for copy in wx2 + wy2:
        copy.wait_recv()
    total_a = wxs[y].astype(F32)
    total_b = wys[x].astype(F32)
    for d in (1, 2, 3):
        total_a += wx2r[d - 1].astype(F32)
        total_b += wy2r[d - 1].astype(F32)
    wdsend[0:RA] = total_a.astype(BF)
    wdsend[RA:T] = total_b.astype(BF)
    wd = go("wd", 0, wdsend, wdrecv, twin)

    for copy in gx:
        copy.wait_recv()
    gyb[y] = gxb[0] + gxb[1] + gxb[2] + gxb[3]
    gy = [go("gy", d - 1, gyb.at[y], gyb.at[y], Y(d)) for d in (1, 2, 3)]

    def wait_grads(h, carry):
        for d in (1, 2, 3):
            kv_copy("dv", h, d, dvs, dvr).wait_recv()
            kv_copy("dk", h, d, dks, dkr).wait_recv()
            q_copy(h, d).wait_recv()
        return carry

    lax.fori_loop(0, NH, wait_grads, 0)
    for out, own, got, index in ((gv_ref, dvs, dvr, y), (gk_ref, dks, dkr, y), (gq_ref, dqs, dqr, x)):
        total = own[index].astype(F32)
        for d in (1, 2, 3):
            total += got[d - 1].astype(F32)
        out[...] = total.astype(BF)

    wd.wait_recv()
    gw_ref[...] = wdsend[...].astype(F32) + wdrecv[...].astype(F32)
    for copy in gy:
        copy.wait_recv()
    gg_ref[...] = (gyb[0] + gyb[1] + gyb[2] + gyb[3])[0:1, :]

    def wait_sends(h, carry):
        for d in (1, 2, 3):
            o_copy(h, d).wait_send()
            kv_copy("dv", h, d, dvs, dvr).wait_send()
            kv_copy("dk", h, d, dks, dkr).wait_send()
            q_copy(h, d).wait_send()
        return carry

    lax.fori_loop(0, NH, wait_sends, 0)
    for copy in sent:
        copy.wait_send()


def shards(query_rows, key_rows, value_rows, lengths, out_weight, gate_vector, cotangent):
    T, DL = query_rows.shape[1:]
    NH = DL // HD
    Q = NX * T
    RA = T // 3
    D = gate_vector.shape[1]

    def vm(shape, dtype=BF):
        return pltpu.VMEM(shape, dtype)

    blocks = (4, T, DL)
    three = (3, T, DL)
    scratch = [
        vm(blocks), vm(blocks), vm(blocks), vm((2 * NZ, T, DL)), vm((NY, NX, T, DL)),
        vm((NH, NY, T, Q), F32), vm((NY, T, Q)), vm((8, Q), F32), vm((NX, 8, Q), F32),
        vm((8, Q), F32), vm((HD, Q), F32), vm((Q, HD), F32),
        vm(blocks), vm(blocks), vm((T, DL)), vm(blocks), vm((T, DL), F32),
        vm(blocks), vm(blocks), vm(blocks, F32), vm(blocks), vm(three),
        vm((NY, NX, T, DL)), vm((3, NY, RA, DL)), vm((3, NX, T - RA, DL)),
        vm((NY, RA, DL)), vm((NX, T - RA, DL)), vm((3, RA, DL)), vm((3, T - RA, DL)),
        vm((T, DL)), vm((T, DL)), vm((NX, 8, Q), F32), vm((8, Q), F32),
        vm(blocks), vm(three), vm(blocks), vm(three), vm(blocks), vm(three), vm((HD, Q), F32),
        vm((NX, 8, DL), F32), vm((NY, 8, DL), F32),
        pltpu.SemaphoreType.DMA((SEM_COUNT,)), pltpu.SemaphoreType.DMA((SEM_COUNT,)),
    ]
    vmem = pl.BlockSpec(memory_space=pltpu.VMEM)
    rows = jax.ShapeDtypeStruct((T, DL), BF)
    outs = pl.pallas_call(
        kernel,
        out_shape=(
            rows, rows, rows, rows,
            jax.ShapeDtypeStruct((T, DL), F32),
            jax.ShapeDtypeStruct((1, DL), F32),
        ),
        in_specs=[pl.BlockSpec(memory_space=pltpu.SMEM)] + [vmem] * 6,
        out_specs=(vmem,) * 6,
        scratch_shapes=scratch,
        compiler_params=pltpu.CompilerParams(
            collective_id=0, has_side_effects=True, vmem_limit_bytes=60 * 1024 * 1024
        ),
    )(lengths, query_rows[0], key_rows[0], value_rows[0], out_weight, gate_vector, cotangent[0])
    branch, grad_q, grad_k, grad_v, grad_w, grad_g = outs
    return branch[None], grad_q[None], grad_k[None], grad_v[None], grad_w, grad_g


def solution(mesh):
    rows = P("dp", "seq", "tensor")
    placed = (rows, rows, rows, P("dp"), P("seq", "tensor"), P("dp", None), rows)
    return jax.shard_map(
        shards,
        mesh=mesh,
        in_specs=placed,
        out_specs=(rows, rows, rows, rows, P("seq", "tensor"), P("dp", "tensor")),
        check_vma=False,
    )
```

time: 501 us -> 97.2 us (0.19)
  waiting for transfers between devices: 332 us -> 0 us
  Pallas kernels: 0 us -> 90.5 us
  blocking collectives: 66.6 us -> 0 us
  local copies, waits for them, and re-layouts: 41.4 us -> 5.2 us
  matrix products: 25.5 us -> 0 us
  other arithmetic: 18.9 us -> 0 us
  between operations: 14.1 us -> 1.3 us
    all_gather x6 -> x0, waiting for transfers between devices: 287 us -> none  [the longest x1 53.2 us: shards(): query_piece = lax.all_gather(query_local, 'seq', axis=0, tiled=True)]
    pallas_call x0 -> x1, Pallas kernels: none -> 90.5 us  [shards(): pl.pallas_call(kernel, out_shape=(rows, rows, rows, rows, jax.ShapeDtypeS...]
    all_gather x2 -> x0, blocking collectives: 35 us -> none  [the longest x1 17.8 us: shards(): lax.all_gather(row_lse, 'seq', axis=0, tiled=True)]
    psum x1 -> x0, blocking collectives: 31.6 us -> none  [shards(): gate_grad = lax.psum(jnp.sum(cot_rows * projected, axis=0), 'seq')]
    reduce_scatter x1 -> x0, waiting for transfers between devices: 30.2 us -> none  [shards(): lax.psum_scatter(jnp.einsum('tr,tk->rk', grad_full, attended, preferred_e...]
    dot_general x45 -> x0, matrix products: 25.5 us -> none  [the longest x6 4.05 us: query_terms(): jnp.einsum('ths,shd->thd', dscores, key_block, preferred_element_type=jnp...]
    dynamic_slice x37 -> x0, local copies, waits for them, and re-layouts: 23.8 us -> none  [the longest x12 8.36 us: key_block_step(): lax.dynamic_slice_in_dim(grad_piece, offset, key_step_rows, 0)]
    psum x1 -> x0, waiting for transfers between devices: 12.5 us -> none  [shards(): grad_weight = lax.psum(row_share, 'dp').astype(jnp.float32)]
  transfers between devices with their start and end apart: 9 -> 0, of which waited for: 8 -> 0; matrix products, arithmetic and copies ran while one was open for 11% -> 0% of each run, Pallas kernels for 0% -> 0%
where the time goes in v1:
time: 97.2 us; the launch traced here: 97 us
  Pallas kernels  90.5 us (93%)
  local copies, waits for them, and re-layouts  5.2 us (5%)
  between operations  1.3 us (1%)
    pallas_call x1, Pallas kernels, shards(): pl.pallas_call(kernel, out_shape=(rows, rows, rows, rows, jax.ShapeDtypeS...  90.5 us
    unnamed x16, local copies, waits for them, and re-layouts  5.2 us

profile of v1, /device:TPU:1, one launch (start us, length us, event | category | flops | bytes accessed | tf_op | source)
XLA Modules:
  0.0 97.0 jit_solution(18040128093274711027)
XLA Ops:
  1.3 90.5 %shard_map.118 = (bf16[192,384]{1,0:T(8,128)(2,1)}, bf16[192,384]{1,0:T(8,128)(2,1)}, bf16[192,384]{1,0:T(8,128)(2,1)}, bf16[192,384]{1,0:T(8,128)(2,1)}, f32[192,384]{1,0:T(8,128)}, /*index=5*/f32[1,384]{1,0:T(1,128)}) custom-call(s32[1]{0:T(128)S(6)} %copy.19.len_ref, bf16[192,384]{1,0:T(8,128)(2,1)} %bitcast.8, bf16[192,384]{1,0:T(8,128)(2,1)} %bitcast.9, ...), custom_call_target="tpu_custom_call" | custom-call | tf_op jit(solution)/shard_map/pallas_call | solution.py:439
  91.8 0.0 copy-start.3
  91.8 1.6 %copy.20 = bf16[1,192,384]{2,1,0:T(8,128)(2,1)} copy(bf16[1,192,384]{2,1,0:T(8,128)(2,1)} %bitcast.15) | data formatting | bytes 294912
  93.5 0.0 copy-done.3
  93.5 0.0 copy-start.2
  93.5 0.0 copy-start.1
  93.5 0.7 copy.21
  94.1 0.3 copy-done.2
  94.4 0.0 copy-start
  94.4 0.7 copy.22
  95.1 0.0 copy-done.1
  95.1 0.7 copy.23
  95.8 0.0 copy-done
  95.8 0.0 copy-start.4
  95.8 0.7 copy.24
  96.5 0.0 copy-done.4
  96.5 0.6 copy.25
Async XLA Ops:
  91.8 1.6 %copy-start.3 = (bf16[192,384]{1,0:T(8,128)(2,1)S(1)}, bf16[192,384]{1,0:T(8,128)(2,1)}, u32[]{:S(2)}) copy-start(bf16[192,384]{1,0:T(8,128)(2,1)} %get-tuple-element.13) | copy-start | bytes 442372
  93.5 1.0 copy-start.2
  93.5 1.6 %copy-start.1 = (bf16[192,384]{1,0:T(8,128)(2,1)S(1)}, bf16[192,384]{1,0:T(8,128)(2,1)}, u32[]{:S(2)}) copy-start(bf16[192,384]{1,0:T(8,128)(2,1)} %get-tuple-element.15) | copy-start | bytes 442372
  94.4 1.3 %copy-start = (f32[192,384]{1,0:T(8,128)S(1)}, f32[192,384]{1,0:T(8,128)}, u32[]{:S(2)}) copy-start(f32[192,384]{1,0:T(8,128)} %get-tuple-element.28) | copy-start | bytes 884740
  95.8 0.7 copy-start.4

commit v2 on v1

--- a/solution.py
+++ b/solution.py
@@ -55,7 +55,7 @@
     DL = q_ref.shape[1]
     NH = DL // HD
     Q = NX * T
-    RA = T // 3
+    RA = T // 2
     scale = 1.0 / math.sqrt(HD)
     seq = lax.axis_index("seq")
     ten = lax.axis_index("tensor")
@@ -409,11 +409,16 @@
         copy.wait_send()
 
 
+def place(*refs):
+    for i in range(6):
+        refs[6 + i][...] = refs[i][...]
+
+
 def shards(query_rows, key_rows, value_rows, lengths, out_weight, gate_vector, cotangent):
     T, DL = query_rows.shape[1:]
     NH = DL // HD
     Q = NX * T
-    RA = T // 3
+    RA = T // 2
     D = gate_vector.shape[1]
 
     def vm(shape, dtype=BF):
@@ -450,7 +455,12 @@
             collective_id=0, has_side_effects=True, vmem_limit_bytes=60 * 1024 * 1024
         ),
     )(lengths, query_rows[0], key_rows[0], value_rows[0], out_weight, gate_vector, cotangent[0])
-    branch, grad_q, grad_k, grad_v, grad_w, grad_g = outs
+    branch, grad_q, grad_k, grad_v, grad_w, grad_g = pl.pallas_call(
+        place,
+        out_shape=tuple(jax.ShapeDtypeStruct(out.shape, out.dtype) for out in outs),
+        in_specs=[vmem] * 6,
+        out_specs=(vmem,) * 6,
+    )(*outs)
     return branch[None], grad_q[None], grad_k[None], grad_v[None], grad_w, grad_g
 
 

time: 97.2 us -> 92.6 us (0.953); the launches traced: 97 us -> 91.1 us
  local copies, waits for them, and re-layouts: 5.2 us -> 0 us
    unnamed x16 -> x0, local copies, waits for them, and re-layouts: 5.2 us -> none
    pallas_call x1, Pallas kernels: 90.5 us -> 87.6 us  [shards(): pl.pallas_call(kernel, out_shape=(rows, rows, rows, rows, jax.ShapeDtypeS...]
    pallas_call x0 -> x1, Pallas kernels: none -> 2.19 us  [shards(): pl.pallas_call(place, out_shape=tuple((jax.ShapeDtypeStruct(out.shape, ou...]
where the time goes in v2:
time: 92.6 us; the launch traced here: 91.1 us
  Pallas kernels  89.8 us (97%)
  between operations  1.29 us (1%)
    pallas_call x1, Pallas kernels, shards(): pl.pallas_call(kernel, out_shape=(rows, rows, rows, rows, jax.ShapeDtypeS...  87.6 us
    pallas_call x1, Pallas kernels, shards(): pl.pallas_call(place, out_shape=tuple((jax.ShapeDtypeStruct(out.shape, ou...  2.19 us

profile of v2, /device:TPU:1, one launch (start us, length us, event | category | flops | bytes accessed | tf_op | source)
XLA Modules:
  0.0 91.1 jit_solution(17773218906633414499)
XLA Ops:
  1.3 87.6 %shard_map.118 = (bf16[192,384]{1,0:T(8,128)(2,1)}, bf16[192,384]{1,0:T(8,128)(2,1)}, bf16[192,384]{1,0:T(8,128)(2,1)}, bf16[192,384]{1,0:T(8,128)(2,1)}, f32[192,384]{1,0:T(8,128)}, /*index=5*/f32[1,384]{1,0:T(1,128)}) custom-call(s32[1]{0:T(128)S(6)} %copy.13.len_ref, bf16[192,384]{1,0:T(8,128)(2,1)} %bitcast.8, bf16[192,384]{1,0:T(8,128)(2,1)} %bitcast.9, ...), custom_call_target="tpu_custom_call" | custom-call | tf_op jit(solution)/shard_map/pallas_call | solution.py:444
  88.9 2.2 %shard_map.119 = (bf16[192,384]{1,0:T(8,128)(2,1)}, bf16[192,384]{1,0:T(8,128)(2,1)}, bf16[192,384]{1,0:T(8,128)(2,1)}, bf16[192,384]{1,0:T(8,128)(2,1)}, f32[192,384]{1,0:T(8,128)}, /*index=5*/f32[1,384]{1,0:T(1,128)}) custom-call(bf16[192,384]{1,0:T(8,128)(2,1)} %get-tuple-element.18.refs_0_, bf16[192,384]{1,0:T(8,128)(2,1)} %get-tuple-element.19.refs_1_, ...), custom_call_target="tpu_custom_call" | custom-call | tf_op jit(solution)/shard_map/pallas_call | solution.py:458

commit v3 on v2

--- a/solution.py
+++ b/solution.py
@@ -35,7 +35,7 @@
 for sem_name, sem_size in (
     ("wa1", 3), ("wb1", 3), ("wa2", 3), ("wb2", 3), ("q", 3), ("k", 3), ("v", 3),
     ("gz", 3), ("gc", 1), ("gf", 3), ("o", 9), ("st", 3), ("do", 3), ("pc", 1), ("pz", 3),
-    ("wx1", 3), ("wy1", 3), ("wx2", 3), ("wy2", 3), ("wd", 1), ("dl", 3),
+    ("ga", 3), ("gb", 1), ("at", 3), ("wx", 3), ("wd", 1), ("dl", 3),
     ("dk", 9), ("dv", 9), ("dq", 9), ("gx", 3), ("gy", 3),
 ):
     SEMS[sem_name] = SEM_COUNT
@@ -47,7 +47,7 @@
     br_ref, gq_ref, gk_ref, gv_ref, gw_ref, gg_ref,
     qbuf, kbuf, vbuf, gfull, wfull, scores, pbuf, top, stat, lse, wrow, wcol,
     osend, orecv, att, dobuf, dacc, psib, psrecv, pown, pzsend, pzrecv,
-    dw, wxr, wyr, wxs, wys, wx2r, wy2r, wdsend, wdrecv, dls, delta,
+    gt, attb, dw, wxr, wdsend, wdrecv, dls, delta,
     dks, dkr, dvs, dvr, dqs, dqr, dqacc, gxb, gyb,
     ss, rs,
 ):
@@ -55,7 +55,7 @@
     DL = q_ref.shape[1]
     NH = DL // HD
     Q = NX * T
-    RA = T // 2
+    RA = T // 6
     scale = 1.0 / math.sqrt(HD)
     seq = lax.axis_index("seq")
     ten = lax.axis_index("tensor")
@@ -164,6 +164,11 @@
         t = zi(NZ - d) * 2 + c
         g_fwd.append(go("gf", d - 1, gfull.at[t], gfull.at[t], sibling))
 
+    g_tile = [
+        go("ga", d - 1, gfull.at[yi(d) * 2 + c], gt.at[c, y], Y(d)) for d in (1, 2, 3)
+    ]
+    gt[c, y] = gfull[y * 2 + c]
+
     for copy in v_in:
         copy.wait_recv()
 
@@ -192,6 +197,10 @@
     lax.fori_loop(0, NH, forward_head, 0)
     st_in = [go("st", d - 1, stat.at[x], stat.at[x], X(d)) for d in (1, 2, 3)]
     orecv[x] = osend[x]
+
+    for copy in g_tile:
+        copy.wait_recv()
+    g_share = go("gb", 0, gt.at[c], gt.at[c], sibling)
 
     for copy in wa2 + wb2 + g_fwd + [g_sib]:
         copy.wait_recv()
@@ -239,6 +248,9 @@
             total += weights[:, col : col + 1] * orecv[j, :, h * HD : (h + 1) * HD].astype(F32)
         att[:, h * HD : (h + 1) * HD] = total.astype(BF)
 
+    attb[y] = att[...]
+    at_in = [go("at", d - 1, att, attb.at[y], Y(d)) for d in (1, 2, 3)]
+
     def proj_sib(z, carry):
         rows = wfull[z, pl.ds((1 - c) * 2, 2)].reshape(2 * T, DL)
         psib[z] = dot_nt(att[...], rows).astype(BF)
@@ -246,15 +258,6 @@
 
     lax.fori_loop(0, NZ, proj_sib, 0)
     p_sib = go("pc", 0, psib, psrecv, sibling)
-
-    def weight_grad(t, carry):
-        part = dot_tn(gfull[t], att[...]).astype(BF).reshape(2, T, DL)
-        dw[lax.div(t, 2), pl.ds(lax.rem(t, 2) * 2, 2)] = part
-        return carry
-
-    lax.fori_loop(0, 2 * NZ, weight_grad, 0)
-    wx1 = [go("wx1", d - 1, dw.at[:, xi(d), 0:RA], wxr.at[d - 1], X(d)) for d in (1, 2, 3)]
-    wy1 = [go("wy1", d - 1, dw.at[yi(d), :, RA:T], wyr.at[d - 1], Y(d)) for d in (1, 2, 3)]
 
     def proj_own(z, carry):
         rows = wfull[z, pl.ds(c * 2, 2)].reshape(2 * T, DL)
@@ -286,6 +289,14 @@
         )
         dls[x, h : h + 1, :] = rows[0:1, :]
     dl_in = [go("dl", d - 1, dls.at[x], dls.at[x], X(d)) for d in (1, 2, 3)]
+
+    for copy in at_in + [g_share]:
+        copy.wait_recv()
+    for half in range(2):
+        part = dot_tn(gt[half].reshape(NY * T, DL), attb[...].reshape(NY * T, DL))
+        dw[2 * half : 2 * half + 2] = part.astype(BF).reshape(2, T, DL)
+    wx = [go("wx", d - 1, dw.at[xi(d)], wxr.at[d - 1], X(d)) for d in (1, 2, 3)]
+
     for copy in dl_in:
         copy.wait_recv()
     for h in range(NH):
@@ -324,30 +335,13 @@
 
     lax.fori_loop(0, NH, backward_head, 0)
 
-    for copy in wx1:
-        copy.wait_recv()
-
-    def sum_x(j, carry):
-        total = dw[j, x, 0:RA].astype(F32)
-        for d in (1, 2, 3):
-            total += wxr[d - 1, j].astype(F32)
-        wxs[j] = total.astype(BF)
-        return carry
-
-    lax.fori_loop(0, NY, sum_x, 0)
-    wx2 = [go("wx2", d - 1, wxs.at[yi(d)], wx2r.at[d - 1], Y(d)) for d in (1, 2, 3)]
-    for copy in wy1:
-        copy.wait_recv()
-
-    def sum_y(j, carry):
-        total = dw[y, j, RA:T].astype(F32)
-        for d in (1, 2, 3):
-            total += wyr[d - 1, j].astype(F32)
-        wys[j] = total.astype(BF)
-        return carry
-
-    lax.fori_loop(0, NX, sum_y, 0)
-    wy2 = [go("wy2", d - 1, wys.at[xi(d)], wy2r.at[d - 1], X(d)) for d in (1, 2, 3)]
+    for copy in wx:
+        copy.wait_recv()
+    total = dw[x].astype(F32)
+    for d in (1, 2, 3):
+        total += wxr[d - 1].astype(F32)
+    wdsend[...] = total.astype(BF)
+    wd = go("wd", 0, wdsend, wdrecv, twin)
 
     for copy in pz:
         copy.wait_recv()
@@ -360,17 +354,6 @@
     )
     gx = [go("gx", d - 1, gxb.at[x], gxb.at[x], X(d)) for d in (1, 2, 3)]
 
-    for copy in wx2 + wy2:
-        copy.wait_recv()
-    total_a = wxs[y].astype(F32)
-    total_b = wys[x].astype(F32)
-    for d in (1, 2, 3):
-        total_a += wx2r[d - 1].astype(F32)
-        total_b += wy2r[d - 1].astype(F32)
-    wdsend[0:RA] = total_a.astype(BF)
-    wdsend[RA:T] = total_b.astype(BF)
-    wd = go("wd", 0, wdsend, wdrecv, twin)
-
     for copy in gx:
         copy.wait_recv()
     gyb[y] = gxb[0] + gxb[1] + gxb[2] + gxb[3]
@@ -418,8 +401,6 @@
     T, DL = query_rows.shape[1:]
     NH = DL // HD
     Q = NX * T
-    RA = T // 2
-    D = gate_vector.shape[1]
 
     def vm(shape, dtype=BF):
         return pltpu.VMEM(shape, dtype)
@@ -432,8 +413,7 @@
         vm((8, Q), F32), vm((HD, Q), F32), vm((Q, HD), F32),
         vm(blocks), vm(blocks), vm((T, DL)), vm(blocks), vm((T, DL), F32),
         vm(blocks), vm(blocks), vm(blocks, F32), vm(blocks), vm(three),
-        vm((NY, NX, T, DL)), vm((3, NY, RA, DL)), vm((3, NX, T - RA, DL)),
-        vm((NY, RA, DL)), vm((NX, T - RA, DL)), vm((3, RA, DL)), vm((3, T - RA, DL)),
+        vm((2, NY, T, DL)), vm(blocks), vm(blocks), vm(three),
         vm((T, DL)), vm((T, DL)), vm((NX, 8, Q), F32), vm((8, Q), F32),
         vm(blocks), vm(three), vm(blocks), vm(three), vm(blocks), vm(three), vm((HD, Q), F32),
         vm((NX, 8, DL), F32), vm((NY, 8, DL), F32),

time: 92.6 us -> 83.5 us (0.902); the launches traced: 91.1 us -> 83.4 us
  Pallas kernels: 89.8 us -> 82.1 us
    pallas_call x1, Pallas kernels: 87.6 us -> 79.9 us  [shards(): pl.pallas_call(kernel, out_shape=(rows, rows, rows, rows, jax.ShapeDtypeS...]
where the time goes in v3:
time: 83.5 us; the launch traced here: 83.4 us
  Pallas kernels  82.1 us (98%)
  between operations  1.29 us (2%)
    pallas_call x1, Pallas kernels, shards(): pl.pallas_call(kernel, out_shape=(rows, rows, rows, rows, jax.ShapeDtypeS...  79.9 us
    pallas_call x1, Pallas kernels, shards(): pl.pallas_call(place, out_shape=tuple((jax.ShapeDtypeStruct(out.shape, ou...  2.19 us

profile of v3, /device:TPU:1, one launch (start us, length us, event | category | flops | bytes accessed | tf_op | source)
XLA Modules:
  0.0 83.4 jit_solution(15683502148677882804)
XLA Ops:
  1.3 79.9 %shard_map.118 = (bf16[192,384]{1,0:T(8,128)(2,1)}, bf16[192,384]{1,0:T(8,128)(2,1)}, bf16[192,384]{1,0:T(8,128)(2,1)}, bf16[192,384]{1,0:T(8,128)(2,1)}, f32[192,384]{1,0:T(8,128)}, /*index=5*/f32[1,384]{1,0:T(1,128)}) custom-call(s32[1]{0:T(128)S(6)} %copy.13.len_ref, bf16[192,384]{1,0:T(8,128)(2,1)} %bitcast.8, bf16[192,384]{1,0:T(8,128)(2,1)} %bitcast.9, ...), custom_call_target="tpu_custom_call" | custom-call | tf_op jit(solution)/shard_map/pallas_call | solution.py:424
  81.2 2.2 %shard_map.119 = (bf16[192,384]{1,0:T(8,128)(2,1)}, bf16[192,384]{1,0:T(8,128)(2,1)}, bf16[192,384]{1,0:T(8,128)(2,1)}, bf16[192,384]{1,0:T(8,128)(2,1)}, f32[192,384]{1,0:T(8,128)}, /*index=5*/f32[1,384]{1,0:T(1,128)}) custom-call(bf16[192,384]{1,0:T(8,128)(2,1)} %get-tuple-element.18.refs_0_, bf16[192,384]{1,0:T(8,128)(2,1)} %get-tuple-element.19.refs_1_, ...), custom_call_target="tpu_custom_call" | custom-call | tf_op jit(solution)/shard_map/pallas_call | solution.py:438

commit v4 on v3

--- a/solution.py
+++ b/solution.py
@@ -49,13 +49,13 @@
     osend, orecv, att, dobuf, dacc, psib, psrecv, pown, pzsend, pzrecv,
     gt, attb, dw, wxr, wdsend, wdrecv, dls, delta,
     dks, dkr, dvs, dvr, dqs, dqr, dqacc, gxb, gyb,
-    ss, rs,
+    pad, ss, rs, reach,
 ):
     T = q_ref.shape[0]
     DL = q_ref.shape[1]
     NH = DL // HD
     Q = NX * T
-    RA = T // 6
+    RA = T // 3
     scale = 1.0 / math.sqrt(HD)
     seq = lax.axis_index("seq")
     ten = lax.axis_index("tensor")
@@ -105,8 +105,8 @@
         return pl.ds(pl.multiple_of(h * HD, HD), HD)
 
     barrier = pltpu.get_barrier_semaphore()
-    peers = [X(d) for d in (1, 2, 3)] + [Y(d) for d in (1, 2, 3)] + [Z(d) for d in (1, 2, 3)]
-    peers += [sibling, twin]
+    near = {"dp": 1 - dp, "tensor": lax.rem(zh + 2 * dp + NZ - 1, NZ) * 2 + c}
+    peers = [X(d) for d in (1, 2, 3)] + [Y(d) for d in (1, 2, 3)] + [sibling, twin, near]
     for peer in peers:
         pl.semaphore_signal(barrier, inc=1, device_id=peer, device_id_type=MESH)
     gate_local = gate_ref[:, pl.ds(pl.multiple_of(ten * DL, HD), DL)]
@@ -116,6 +116,7 @@
     vbuf[y] = v_ref[...]
     wfull[y, x] = w_ref[...]
     wrow[...] = jnp.zeros_like(wrow)
+    pad[...] = jnp.zeros_like(pad)
     pl.semaphore_wait(barrier, len(peers))
 
     wa1 = [go("wa1", d - 1, w_ref.at[0:RA], wfull.at[y, x, 0:RA], X(d)) for d in (1, 2, 3)]
@@ -123,6 +124,12 @@
     q_in = [go("q", d - 1, q_ref, qbuf.at[x], X(d)) for d in (1, 2, 3)]
     k_in = [go("k", d - 1, k_ref, kbuf.at[y], Y(d)) for d in (1, 2, 3)]
     v_in = [go("v", d - 1, v_ref, vbuf.at[y], Y(d)) for d in (1, 2, 3)]
+    for peer in (twin, near):
+        pl.semaphore_signal(reach.at[0], inc=1, device_id=peer, device_id_type=MESH)
+    pl.semaphore_wait(reach.at[0], 2)
+    for peer in (Z(1), Z(3)):
+        pl.semaphore_signal(reach.at[1], inc=1, device_id=peer, device_id_type=MESH)
+    pl.semaphore_wait(reach.at[1], 2)
     g_in = [go("gz", d - 1, gfull.at[ten], gfull.at[ten], Z(d)) for d in (1, 2, 3)]
     g_sib = go("gc", 0, gfull.at[ten], gfull.at[ten], sibling)
 
@@ -164,11 +171,6 @@
         t = zi(NZ - d) * 2 + c
         g_fwd.append(go("gf", d - 1, gfull.at[t], gfull.at[t], sibling))
 
-    g_tile = [
-        go("ga", d - 1, gfull.at[yi(d) * 2 + c], gt.at[c, y], Y(d)) for d in (1, 2, 3)
-    ]
-    gt[c, y] = gfull[y * 2 + c]
-
     for copy in v_in:
         copy.wait_recv()
 
@@ -198,12 +200,13 @@
     st_in = [go("st", d - 1, stat.at[x], stat.at[x], X(d)) for d in (1, 2, 3)]
     orecv[x] = osend[x]
 
-    for copy in g_tile:
-        copy.wait_recv()
-    g_share = go("gb", 0, gt.at[c], gt.at[c], sibling)
-
     for copy in wa2 + wb2 + g_fwd + [g_sib]:
         copy.wait_recv()
+
+    g_tile = [
+        go("ga", d - 1, gfull.at[yi(d) * 2 + c], gt.at[c, y], Y(d)) for d in (1, 2, 3)
+    ]
+    gt[c, y] = gfull[y * 2 + c]
 
     def weight_rows(t):
         return wfull[lax.div(t, 2), pl.ds(lax.rem(t, 2) * 2, 2)].reshape(2 * T, DL)
@@ -251,6 +254,19 @@
     attb[y] = att[...]
     at_in = [go("at", d - 1, att, attb.at[y], Y(d)) for d in (1, 2, 3)]
 
+    ones = jnp.ones((8, HD), F32)
+    dls[x] = jnp.zeros((8, Q), F32)
+    own_rows = pl.ds(pl.multiple_of(x * T, 64), T)
+    for h in range(NH):
+        sl = slice(h * HD, (h + 1) * HD)
+        pad[own_rows, :] = dobuf[x, :, sl].astype(F32) * att[:, sl].astype(F32)
+        rows = lax.dot_general(
+            ones, pad[...], (((1,), (1,)), ((), ())),
+            preferred_element_type=F32, precision=lax.Precision.HIGHEST,
+        )
+        dls[x, h : h + 1, :] = rows[0:1, :]
+    dl_in = [go("dl", d - 1, dls.at[x], dls.at[x], X(d)) for d in (1, 2, 3)]
+
     def proj_sib(z, carry):
         rows = wfull[z, pl.ds((1 - c) * 2, 2)].reshape(2 * T, DL)
         psib[z] = dot_nt(att[...], rows).astype(BF)
@@ -276,19 +292,12 @@
     lax.fori_loop(0, NZ, proj_add, 0)
     pz = [go("pz", d - 1, pzsend.at[zi(d)], pzrecv.at[d - 1], Z(d)) for d in (1, 2, 3)]
 
+    for copy in g_tile:
+        copy.wait_recv()
+    g_share = go("gb", 0, gt.at[c], gt.at[c], sibling)
+
     for copy in do_in:
         copy.wait_recv()
-    ones = jnp.ones((8, HD), F32)
-    dls[x] = jnp.zeros((8, Q), F32)
-    for h in range(NH):
-        sl = slice(h * HD, (h + 1) * HD)
-        prod = dobuf[:, :, sl].astype(F32) * osend[:, :, sl].astype(F32)
-        rows = lax.dot_general(
-            ones, prod.reshape(Q, HD), (((1,), (1,)), ((), ())),
-            preferred_element_type=F32, precision=lax.Precision.HIGHEST,
-        )
-        dls[x, h : h + 1, :] = rows[0:1, :]
-    dl_in = [go("dl", d - 1, dls.at[x], dls.at[x], X(d)) for d in (1, 2, 3)]
 
     for copy in at_in + [g_share]:
         copy.wait_recv()
@@ -300,9 +309,7 @@
     for copy in dl_in:
         copy.wait_recv()
     for h in range(NH):
-        delta[h : h + 1, :] = sum(
-            wrow[h * NX + j : h * NX + j + 1, :] * dls[j, h : h + 1, :] for j in range(NX)
-        )
+        delta[h : h + 1, :] = sum(dls[j, h : h + 1, :] for j in range(NX))
 
     def kv_copy(name, h, d, src, dst):
         return rc(
@@ -417,7 +424,9 @@
         vm((T, DL)), vm((T, DL)), vm((NX, 8, Q), F32), vm((8, Q), F32),
         vm(blocks), vm(three), vm(blocks), vm(three), vm(blocks), vm(three), vm((HD, Q), F32),
         vm((NX, 8, DL), F32), vm((NY, 8, DL), F32),
+        vm((Q, HD), F32),
         pltpu.SemaphoreType.DMA((SEM_COUNT,)), pltpu.SemaphoreType.DMA((SEM_COUNT,)),
+        pltpu.SemaphoreType.REGULAR((2,)),
     ]
     vmem = pl.BlockSpec(memory_space=pltpu.VMEM)
     rows = jax.ShapeDtypeStruct((T, DL), BF)

time: 83.5 us -> 81.6 us (0.977)
  Pallas kernels: 82.1 us -> 80.1 us
    pallas_call x1, Pallas kernels: 79.9 us -> 77.9 us  [shards(): pl.pallas_call(kernel, out_shape=(rows, rows, rows, rows, jax.ShapeDtypeS...]
where the time goes in v4:
time: 81.6 us; the launch traced here: 81.4 us
  Pallas kernels  80.1 us (98%)
  between operations  1.29 us (2%)
    pallas_call x1, Pallas kernels, shards(): pl.pallas_call(kernel, out_shape=(rows, rows, rows, rows, jax.ShapeDtypeS...  77.9 us
    pallas_call x1, Pallas kernels, shards(): pl.pallas_call(place, out_shape=tuple((jax.ShapeDtypeStruct(out.shape, ou...  2.19 us

profile of v4, /device:TPU:1, one launch (start us, length us, event | category | flops | bytes accessed | tf_op | source)
XLA Modules:
  0.0 81.4 jit_solution(6091523391350894378)
XLA Ops:
  1.3 77.9 %shard_map.118 = (bf16[192,384]{1,0:T(8,128)(2,1)}, bf16[192,384]{1,0:T(8,128)(2,1)}, bf16[192,384]{1,0:T(8,128)(2,1)}, bf16[192,384]{1,0:T(8,128)(2,1)}, f32[192,384]{1,0:T(8,128)}, /*index=5*/f32[1,384]{1,0:T(1,128)}) custom-call(s32[1]{0:T(128)S(6)} %copy.13.len_ref, bf16[192,384]{1,0:T(8,128)(2,1)} %bitcast.8, bf16[192,384]{1,0:T(8,128)(2,1)} %bitcast.9, ...), custom_call_target="tpu_custom_call" | custom-call | tf_op jit(solution)/shard_map/pallas_call | solution.py:433
  79.2 2.2 %shard_map.119 = (bf16[192,384]{1,0:T(8,128)(2,1)}, bf16[192,384]{1,0:T(8,128)(2,1)}, bf16[192,384]{1,0:T(8,128)(2,1)}, bf16[192,384]{1,0:T(8,128)(2,1)}, f32[192,384]{1,0:T(8,128)}, /*index=5*/f32[1,384]{1,0:T(1,128)}) custom-call(bf16[192,384]{1,0:T(8,128)(2,1)} %get-tuple-element.18.refs_0_, bf16[192,384]{1,0:T(8,128)(2,1)} %get-tuple-element.19.refs_1_, ...), custom_call_target="tpu_custom_call" | custom-call | tf_op jit(solution)/shard_map/pallas_call | solution.py:447

commit v5 on v4

--- a/solution.py
+++ b/solution.py
@@ -254,18 +254,19 @@
     attb[y] = att[...]
     at_in = [go("at", d - 1, att, attb.at[y], Y(d)) for d in (1, 2, 3)]
 
-    ones = jnp.ones((8, HD), F32)
-    dls[x] = jnp.zeros((8, Q), F32)
-    own_rows = pl.ds(pl.multiple_of(x * T, 64), T)
+    lane = lax.broadcasted_iota(jnp.int32, (T, HD), 1)
+    columns = jnp.zeros((T, HD), F32)
     for h in range(NH):
         sl = slice(h * HD, (h + 1) * HD)
-        pad[own_rows, :] = dobuf[x, :, sl].astype(F32) * att[:, sl].astype(F32)
-        rows = lax.dot_general(
-            ones, pad[...], (((1,), (1,)), ((), ())),
-            preferred_element_type=F32, precision=lax.Precision.HIGHEST,
-        )
-        dls[x, h : h + 1, :] = rows[0:1, :]
+        prod = dobuf[x, :, sl].astype(F32) * att[:, sl].astype(F32)
+        columns = jnp.where(lane == h, jnp.sum(prod, axis=1, keepdims=True), columns)
+    pad[pl.ds(pl.multiple_of(x * T, 64), T), :] = columns
+    dls[x] = pad[...].T[0:8, :]
     dl_in = [go("dl", d - 1, dls.at[x], dls.at[x], X(d)) for d in (1, 2, 3)]
+
+    for copy in g_tile:
+        copy.wait_recv()
+    g_share = go("gb", 0, gt.at[c], gt.at[c], sibling)
 
     def proj_sib(z, carry):
         rows = wfull[z, pl.ds((1 - c) * 2, 2)].reshape(2 * T, DL)
@@ -292,19 +293,8 @@
     lax.fori_loop(0, NZ, proj_add, 0)
     pz = [go("pz", d - 1, pzsend.at[zi(d)], pzrecv.at[d - 1], Z(d)) for d in (1, 2, 3)]
 
-    for copy in g_tile:
-        copy.wait_recv()
-    g_share = go("gb", 0, gt.at[c], gt.at[c], sibling)
-
     for copy in do_in:
         copy.wait_recv()
-
-    for copy in at_in + [g_share]:
-        copy.wait_recv()
-    for half in range(2):
-        part = dot_tn(gt[half].reshape(NY * T, DL), attb[...].reshape(NY * T, DL))
-        dw[2 * half : 2 * half + 2] = part.astype(BF).reshape(2, T, DL)
-    wx = [go("wx", d - 1, dw.at[xi(d)], wxr.at[d - 1], X(d)) for d in (1, 2, 3)]
 
     for copy in dl_in:
         copy.wait_recv()
@@ -340,7 +330,16 @@
             q_copy(h, d).start()
         return carry
 
-    lax.fori_loop(0, NH, backward_head, 0)
+    lax.fori_loop(0, 1, backward_head, 0)
+
+    for copy in at_in + [g_share]:
+        copy.wait_recv()
+    for half in range(2):
+        part = dot_tn(gt[half].reshape(NY * T, DL), attb[...].reshape(NY * T, DL))
+        dw[2 * half : 2 * half + 2] = part.astype(BF).reshape(2, T, DL)
+    wx = [go("wx", d - 1, dw.at[xi(d)], wxr.at[d - 1], X(d)) for d in (1, 2, 3)]
+
+    lax.fori_loop(1, NH, backward_head, 0)
 
     for copy in wx:
         copy.wait_recv()

time: 81.6 us -> 80.8 us (level)
  no operation moved by 1% of the time
where the time goes in v5:
time: 80.8 us; the launch traced here: 80.6 us
  Pallas kernels  79.3 us (98%)
  between operations  1.29 us (2%)
    pallas_call x1, Pallas kernels, shards(): pl.pallas_call(kernel, out_shape=(rows, rows, rows, rows, jax.ShapeDtypeS...  77.1 us
    pallas_call x1, Pallas kernels, shards(): pl.pallas_call(place, out_shape=tuple((jax.ShapeDtypeStruct(out.shape, ou...  2.19 us

profile of v5, /device:TPU:1, one launch (start us, length us, event | category | flops | bytes accessed | tf_op | source)
XLA Modules:
  0.0 80.6 jit_solution(15770526932753351756)
XLA Ops:
  1.3 77.1 %shard_map.118 = (bf16[192,384]{1,0:T(8,128)(2,1)}, bf16[192,384]{1,0:T(8,128)(2,1)}, bf16[192,384]{1,0:T(8,128)(2,1)}, bf16[192,384]{1,0:T(8,128)(2,1)}, f32[192,384]{1,0:T(8,128)}, /*index=5*/f32[1,384]{1,0:T(1,128)}) custom-call(s32[1]{0:T(128)S(6)} %copy.13.len_ref, bf16[192,384]{1,0:T(8,128)(2,1)} %bitcast.8, bf16[192,384]{1,0:T(8,128)(2,1)} %bitcast.9, ...), custom_call_target="tpu_custom_call" | custom-call | tf_op jit(solution)/shard_map/pallas_call | solution.py:432
  78.4 2.2 %shard_map.119 = (bf16[192,384]{1,0:T(8,128)(2,1)}, bf16[192,384]{1,0:T(8,128)(2,1)}, bf16[192,384]{1,0:T(8,128)(2,1)}, bf16[192,384]{1,0:T(8,128)(2,1)}, f32[192,384]{1,0:T(8,128)}, /*index=5*/f32[1,384]{1,0:T(1,128)}) custom-call(bf16[192,384]{1,0:T(8,128)(2,1)} %get-tuple-element.18.refs_0_, bf16[192,384]{1,0:T(8,128)(2,1)} %get-tuple-element.19.refs_1_, ...), custom_call_target="tpu_custom_call" | custom-call | tf_op jit(solution)/shard_map/pallas_call | solution.py:446

commit v6 on v5

--- a/solution.py
+++ b/solution.py
@@ -34,9 +34,9 @@
 SEM_COUNT = 0
 for sem_name, sem_size in (
     ("wa1", 3), ("wb1", 3), ("wa2", 3), ("wb2", 3), ("q", 3), ("k", 3), ("v", 3),
-    ("gz", 3), ("gc", 1), ("gf", 3), ("o", 9), ("st", 3), ("do", 3), ("pc", 1), ("pz", 3),
+    ("gz", 3), ("gc", 1), ("gf", 3), ("o", 9), ("st", 3), ("do", 3), ("pc", 4), ("pz", 3),
     ("ga", 3), ("gb", 1), ("at", 3), ("wx", 3), ("wd", 1), ("dl", 3),
-    ("dk", 9), ("dv", 9), ("dq", 9), ("gx", 3), ("gy", 3),
+    ("dk", 9), ("dv", 9), ("dq", 9), ("gx", 15),
 ):
     SEMS[sem_name] = SEM_COUNT
     SEM_COUNT += sem_size
@@ -48,7 +48,7 @@
     qbuf, kbuf, vbuf, gfull, wfull, scores, pbuf, top, stat, lse, wrow, wcol,
     osend, orecv, att, dobuf, dacc, psib, psrecv, pown, pzsend, pzrecv,
     gt, attb, dw, wxr, wdsend, wdrecv, dls, delta,
-    dks, dkr, dvs, dvr, dqs, dqr, dqacc, gxb, gyb,
+    dks, dkr, dvs, dvr, dqs, dqr, dqacc, gxb,
     pad, ss, rs, reach,
 ):
     T = q_ref.shape[0]
@@ -251,8 +251,28 @@
             total += weights[:, col : col + 1] * orecv[j, :, h * HD : (h + 1) * HD].astype(F32)
         att[:, h * HD : (h + 1) * HD] = total.astype(BF)
 
+    p_sib = {}
+    for d in (2, 1, 3, 0):
+        z = zi(d)
+        rows = wfull[z, pl.ds((1 - c) * 2, 2)].reshape(2 * T, DL)
+        psib[z] = dot_nt(att[...], rows).astype(BF)
+        p_sib[d] = go("pc", d, psib.at[z], psrecv.at[z], sibling)
+
     attb[y] = att[...]
     at_in = [go("at", d - 1, att, attb.at[y], Y(d)) for d in (1, 2, 3)]
+
+    pz = []
+    for d in (2, 1, 3, 0):
+        z = zi(d)
+        rows = wfull[z, pl.ds(c * 2, 2)].reshape(2 * T, DL)
+        value = dot_nt(att[...], rows)
+        p_sib[d].wait_recv()
+        value += psrecv[z].astype(F32)
+        if d:
+            pzsend[z] = value.astype(BF)
+            pz.append(go("pz", d - 1, pzsend.at[z], pzrecv.at[d - 1], Z(d)))
+        else:
+            pown[...] = value
 
     lane = lax.broadcasted_iota(jnp.int32, (T, HD), 1)
     columns = jnp.zeros((T, HD), F32)
@@ -267,31 +287,6 @@
     for copy in g_tile:
         copy.wait_recv()
     g_share = go("gb", 0, gt.at[c], gt.at[c], sibling)
-
-    def proj_sib(z, carry):
-        rows = wfull[z, pl.ds((1 - c) * 2, 2)].reshape(2 * T, DL)
-        psib[z] = dot_nt(att[...], rows).astype(BF)
-        return carry
-
-    lax.fori_loop(0, NZ, proj_sib, 0)
-    p_sib = go("pc", 0, psib, psrecv, sibling)
-
-    def proj_own(z, carry):
-        rows = wfull[z, pl.ds(c * 2, 2)].reshape(2 * T, DL)
-        pown[z] = dot_nt(att[...], rows)
-        return carry
-
-    lax.fori_loop(0, NZ, proj_own, 0)
-    p_sib.wait_recv()
-
-    def proj_add(z, carry):
-        value = pown[z] + psrecv[z].astype(F32)
-        pown[z] = value
-        pzsend[z] = value.astype(BF)
-        return carry
-
-    lax.fori_loop(0, NZ, proj_add, 0)
-    pz = [go("pz", d - 1, pzsend.at[zi(d)], pzrecv.at[d - 1], Z(d)) for d in (1, 2, 3)]
 
     for copy in do_in:
         copy.wait_recv()
@@ -351,19 +346,17 @@
 
     for copy in pz:
         copy.wait_recv()
-    projected = pown[zh]
+    projected = pown[...]
     for d in (1, 2, 3):
         projected += pzrecv[d - 1].astype(F32)
     br_ref[...] = (gate_local * projected).astype(BF)
-    gxb[x] = jnp.broadcast_to(
+    gxb[seq] = jnp.broadcast_to(
         jnp.sum(cot_ref[...].astype(F32) * projected, axis=0, keepdims=True), (8, DL)
     )
-    gx = [go("gx", d - 1, gxb.at[x], gxb.at[x], X(d)) for d in (1, 2, 3)]
-
-    for copy in gx:
-        copy.wait_recv()
-    gyb[y] = gxb[0] + gxb[1] + gxb[2] + gxb[3]
-    gy = [go("gy", d - 1, gyb.at[y], gyb.at[y], Y(d)) for d in (1, 2, 3)]
+    gx = [
+        go("gx", n - 1, gxb.at[seq], gxb.at[seq], {"seq": yi(n // NX) * NX + xi(n % NX)})
+        for n in range(1, NX * NY)
+    ]
 
     def wait_grads(h, carry):
         for d in (1, 2, 3):
@@ -381,9 +374,9 @@
 
     wd.wait_recv()
     gw_ref[...] = wdsend[...].astype(F32) + wdrecv[...].astype(F32)
-    for copy in gy:
-        copy.wait_recv()
-    gg_ref[...] = (gyb[0] + gyb[1] + gyb[2] + gyb[3])[0:1, :]
+    for copy in gx:
+        copy.wait_recv()
+    gg_ref[...] = sum(gxb[n] for n in range(NX * NY))[0:1, :]
 
     def wait_sends(h, carry):
         for d in (1, 2, 3):
@@ -418,11 +411,11 @@
         vm((NH, NY, T, Q), F32), vm((NY, T, Q)), vm((8, Q), F32), vm((NX, 8, Q), F32),
         vm((8, Q), F32), vm((HD, Q), F32), vm((Q, HD), F32),
         vm(blocks), vm(blocks), vm((T, DL)), vm(blocks), vm((T, DL), F32),
-        vm(blocks), vm(blocks), vm(blocks, F32), vm(blocks), vm(three),
+        vm(blocks), vm(blocks), vm((T, DL), F32), vm(blocks), vm(three),
         vm((2, NY, T, DL)), vm(blocks), vm(blocks), vm(three),
         vm((T, DL)), vm((T, DL)), vm((NX, 8, Q), F32), vm((8, Q), F32),
         vm(blocks), vm(three), vm(blocks), vm(three), vm(blocks), vm(three), vm((HD, Q), F32),
-        vm((NX, 8, DL), F32), vm((NY, 8, DL), F32),
+        vm((NX * NY, 8, DL), F32),
         vm((Q, HD), F32),
         pltpu.SemaphoreType.DMA((SEM_COUNT,)), pltpu.SemaphoreType.DMA((SEM_COUNT,)),
         pltpu.SemaphoreType.REGULAR((2,)),

time: 80.8 us -> 80 us (0.990)
  no operation moved by 1% of the time
where the time goes in v6:
time: 80 us; the launch traced here: 79.9 us
  Pallas kernels  78.6 us (98%)
  between operations  1.29 us (2%)
    pallas_call x1, Pallas kernels, shards(): pl.pallas_call(kernel, out_shape=(rows, rows, rows, rows, jax.ShapeDtypeS...  76.4 us
    pallas_call x1, Pallas kernels, shards(): pl.pallas_call(place, out_shape=tuple((jax.ShapeDtypeStruct(out.shape, ou...  2.19 us

profile of v6, /device:TPU:1, one launch (start us, length us, event | category | flops | bytes accessed | tf_op | source)
XLA Modules:
  0.0 79.9 jit_solution(16929658167955054348)
XLA Ops:
  1.3 76.4 %shard_map.118 = (bf16[192,384]{1,0:T(8,128)(2,1)}, bf16[192,384]{1,0:T(8,128)(2,1)}, bf16[192,384]{1,0:T(8,128)(2,1)}, bf16[192,384]{1,0:T(8,128)(2,1)}, f32[192,384]{1,0:T(8,128)}, /*index=5*/f32[1,384]{1,0:T(1,128)}) custom-call(s32[1]{0:T(128)S(6)} %copy.13.len_ref, bf16[192,384]{1,0:T(8,128)(2,1)} %bitcast.8, bf16[192,384]{1,0:T(8,128)(2,1)} %bitcast.9, ...), custom_call_target="tpu_custom_call" | custom-call | tf_op jit(solution)/shard_map/pallas_call | solution.py:425
  77.7 2.2 %shard_map.119 = (bf16[192,384]{1,0:T(8,128)(2,1)}, bf16[192,384]{1,0:T(8,128)(2,1)}, bf16[192,384]{1,0:T(8,128)(2,1)}, bf16[192,384]{1,0:T(8,128)(2,1)}, f32[192,384]{1,0:T(8,128)}, /*index=5*/f32[1,384]{1,0:T(1,128)}) custom-call(bf16[192,384]{1,0:T(8,128)(2,1)} %get-tuple-element.18.refs_0_, bf16[192,384]{1,0:T(8,128)(2,1)} %get-tuple-element.19.refs_1_, ...), custom_call_target="tpu_custom_call" | custom-call | tf_op jit(solution)/shard_map/pallas_call | solution.py:439

commit v7 on v6

--- a/solution.py
+++ b/solution.py
@@ -55,7 +55,7 @@
     DL = q_ref.shape[1]
     NH = DL // HD
     Q = NX * T
-    RA = T // 3
+    RA = T // 2
     scale = 1.0 / math.sqrt(HD)
     seq = lax.axis_index("seq")
     ten = lax.axis_index("tensor")
@@ -336,14 +336,6 @@
 
     lax.fori_loop(1, NH, backward_head, 0)
 
-    for copy in wx:
-        copy.wait_recv()
-    total = dw[x].astype(F32)
-    for d in (1, 2, 3):
-        total += wxr[d - 1].astype(F32)
-    wdsend[...] = total.astype(BF)
-    wd = go("wd", 0, wdsend, wdrecv, twin)
-
     for copy in pz:
         copy.wait_recv()
     projected = pown[...]
@@ -357,6 +349,14 @@
         go("gx", n - 1, gxb.at[seq], gxb.at[seq], {"seq": yi(n // NX) * NX + xi(n % NX)})
         for n in range(1, NX * NY)
     ]
+
+    for copy in wx:
+        copy.wait_recv()
+    total = dw[x].astype(F32)
+    for d in (1, 2, 3):
+        total += wxr[d - 1].astype(F32)
+    wdsend[...] = total.astype(BF)
+    wd = go("wd", 0, wdsend, wdrecv, twin)
 
     def wait_grads(h, carry):
         for d in (1, 2, 3):

time: 80 us -> 78 us (0.975)
  Pallas kernels: 78.6 us -> 76.4 us
    pallas_call x1, Pallas kernels: 76.4 us -> 74.2 us  [shards(): pl.pallas_call(kernel, out_shape=(rows, rows, rows, rows, jax.ShapeDtypeS...]
where the time goes in v7:
time: 78 us; the launch traced here: 77.7 us
  Pallas kernels  76.4 us (98%)
  between operations  1.29 us (2%)
    pallas_call x1, Pallas kernels, shards(): pl.pallas_call(kernel, out_shape=(rows, rows, rows, rows, jax.ShapeDtypeS...  74.2 us
    pallas_call x1, Pallas kernels, shards(): pl.pallas_call(place, out_shape=tuple((jax.ShapeDtypeStruct(out.shape, ou...  2.19 us

profile of v7, /device:TPU:1, one launch (start us, length us, event | category | flops | bytes accessed | tf_op | source)
XLA Modules:
  0.0 77.7 jit_solution(14901535035063534197)
XLA Ops:
  1.3 74.2 %shard_map.118 = (bf16[192,384]{1,0:T(8,128)(2,1)}, bf16[192,384]{1,0:T(8,128)(2,1)}, bf16[192,384]{1,0:T(8,128)(2,1)}, bf16[192,384]{1,0:T(8,128)(2,1)}, f32[192,384]{1,0:T(8,128)}, /*index=5*/f32[1,384]{1,0:T(1,128)}) custom-call(s32[1]{0:T(128)S(6)} %copy.13.len_ref, bf16[192,384]{1,0:T(8,128)(2,1)} %bitcast.8, bf16[192,384]{1,0:T(8,128)(2,1)} %bitcast.9, ...), custom_call_target="tpu_custom_call" | custom-call | tf_op jit(solution)/shard_map/pallas_call | solution.py:425
  75.5 2.2 %shard_map.119 = (bf16[192,384]{1,0:T(8,128)(2,1)}, bf16[192,384]{1,0:T(8,128)(2,1)}, bf16[192,384]{1,0:T(8,128)(2,1)}, bf16[192,384]{1,0:T(8,128)(2,1)}, f32[192,384]{1,0:T(8,128)}, /*index=5*/f32[1,384]{1,0:T(1,128)}) custom-call(bf16[192,384]{1,0:T(8,128)(2,1)} %get-tuple-element.18.refs_0_, bf16[192,384]{1,0:T(8,128)(2,1)} %get-tuple-element.19.refs_1_, ...), custom_call_target="tpu_custom_call" | custom-call | tf_op jit(solution)/shard_map/pallas_call | solution.py:439

commit v8 on v7

--- a/solution.py
+++ b/solution.py
@@ -55,7 +55,7 @@
     DL = q_ref.shape[1]
     NH = DL // HD
     Q = NX * T
-    RA = T // 2
+    RA = T * 5 // 12
     scale = 1.0 / math.sqrt(HD)
     seq = lax.axis_index("seq")
     ten = lax.axis_index("tensor")

time: 78 us -> 78.2 us (level)
  no operation moved by 1% of the time
where the time goes in v8:
time: 78.2 us; the launch traced here: 78.1 us
  Pallas kernels  76.8 us (98%)
  between operations  1.29 us (2%)
    pallas_call x1, Pallas kernels, shards(): pl.pallas_call(kernel, out_shape=(rows, rows, rows, rows, jax.ShapeDtypeS...  74.6 us
    pallas_call x1, Pallas kernels, shards(): pl.pallas_call(place, out_shape=tuple((jax.ShapeDtypeStruct(out.shape, ou...  2.19 us

profile of v8, /device:TPU:1, one launch (start us, length us, event | category | flops | bytes accessed | tf_op | source)
XLA Modules:
  0.0 78.1 jit_solution(13405293784536514641)
XLA Ops:
  1.3 74.6 %shard_map.118 = (bf16[192,384]{1,0:T(8,128)(2,1)}, bf16[192,384]{1,0:T(8,128)(2,1)}, bf16[192,384]{1,0:T(8,128)(2,1)}, bf16[192,384]{1,0:T(8,128)(2,1)}, f32[192,384]{1,0:T(8,128)}, /*index=5*/f32[1,384]{1,0:T(1,128)}) custom-call(s32[1]{0:T(128)S(6)} %copy.13.len_ref, bf16[192,384]{1,0:T(8,128)(2,1)} %bitcast.8, bf16[192,384]{1,0:T(8,128)(2,1)} %bitcast.9, ...), custom_call_target="tpu_custom_call" | custom-call | tf_op jit(solution)/shard_map/pallas_call | solution.py:425
  75.9 2.2 %shard_map.119 = (bf16[192,384]{1,0:T(8,128)(2,1)}, bf16[192,384]{1,0:T(8,128)(2,1)}, bf16[192,384]{1,0:T(8,128)(2,1)}, bf16[192,384]{1,0:T(8,128)(2,1)}, f32[192,384]{1,0:T(8,128)}, /*index=5*/f32[1,384]{1,0:T(1,128)}) custom-call(bf16[192,384]{1,0:T(8,128)(2,1)} %get-tuple-element.18.refs_0_, bf16[192,384]{1,0:T(8,128)(2,1)} %get-tuple-element.19.refs_1_, ...), custom_call_target="tpu_custom_call" | custom-call | tf_op jit(solution)/shard_map/pallas_call | solution.py:439
